TPU v7x, 32 devices: a whole 2x2x4 slice. The times are simulated.
32 devices in a mesh: ens: 4 (over y, x), space: 8 (over z, core).
Axes of the slice: x: 2, y: 2, z: 4, core: 2. Of those that a mesh axis runs over, the one named last changes fastest.
Arguments:
- latent: bfloat16 [16, 256, 8192], P('ens', None, 'space'), may hold values from -6 to 6
- noise: bfloat16 [16, 256, 8192], P('ens', None, 'space'), may hold values from -6 to 6
- target: float32 [224, 8192], P('ens', 'space'), may hold values from -6 to 6
- w_in: bfloat16 [384, 256], replicated, may hold values from -0.375 to 0.375
- w_out: bfloat16 [224, 384], replicated, may hold values from -0.3125 to 0.3125
- w_close_in: bfloat16 [384, 224], replicated, may hold values from -0.375 to 0.375
- w_close_out: bfloat16 [224, 384], replicated, may hold values from -0.3125 to 0.3125
Outputs:
- grad_latent: float32 [16, 256, 8192], P('ens', None, 'space')
- step_in: float32 [384, 256], replicated
- step_out: float32 [224, 384], replicated
- step_close_in: float32 [384, 224], replicated
- step_close_out: float32 [224, 384], replicated
All inputs are finite; a program needn't handle non-finite values.
Results may differ from a plain program's by a relative error of at most 0.011.
Values sent between devices are 32-bit elements; how exact they have to be, the bound alone decides.
A program may use at most 128 MiB of HBM per device.

v0:
```python
import jax
import jax.numpy as jnp
from jax import lax
from jax.sharding import PartitionSpec as P

smooth_eps = 0.1


def activate(value):
    return jax.nn.gelu(value, approximate=True)


def activate_back(pre, grad):
    return jax.vjp(activate, pre)[1](grad)[0]


def smooth_sign(diff):
    return diff / jnp.sqrt(diff * diff + smooth_eps * smooth_eps)


def pair_terms(mine, every, truth):
    count = every.shape[0]

    def add_one(index, total):
        other = lax.dynamic_index_in_dim(every, index, 0, keepdims=False)
        return total + smooth_sign(mine - other)

    total = lax.fori_loop(0, count, add_one, jnp.zeros_like(mine))
    return smooth_sign(mine - truth) - total / count


def body(latent, noise, target, w_in, w_out, w_close_in, w_close_out):
    f32 = jnp.float32
    zin = (latent.astype(f32) + 0.5 * noise.astype(f32)).astype(jnp.bfloat16)
    pre1 = jnp.einsum("hf,mfc->mhc", w_in, zin, preferred_element_type=f32)
    hid1 = activate(pre1).astype(jnp.bfloat16)
    dec = jnp.einsum("kh,mhc->mkc", w_out, hid1, preferred_element_type=f32)
    decb = dec.astype(jnp.bfloat16)
    pre3 = jnp.einsum("hk,mkc->mhc", w_close_in, decb, preferred_element_type=f32)
    hid3 = activate(pre3).astype(jnp.bfloat16)
    pred = dec + jnp.einsum("kh,mhc->mkc", w_close_out, hid3, preferred_element_type=f32)
    every, full_target = (
        lax.all_gather(pred, "ens", axis=0, tiled=True),
        lax.all_gather(target, "ens", axis=0, tiled=True),
    )
    gpred = pair_terms(pred, every, full_target)
    gpredb = gpred.astype(jnp.bfloat16)
    g_close_out = jnp.einsum("mkc,mhc->kh", gpredb, hid3, preferred_element_type=f32)
    g_hid3 = jnp.einsum("kh,mkc->mhc", w_close_out, gpredb, preferred_element_type=f32)
    gpre3 = activate_back(pre3, g_hid3).astype(jnp.bfloat16)
    g_close_in = jnp.einsum("mhc,mkc->hk", gpre3, decb, preferred_element_type=f32)
    gdec = (
        gpred + jnp.einsum("hk,mhc->mkc", w_close_in, gpre3, preferred_element_type=f32)
    ).astype(jnp.bfloat16)
    g_out = jnp.einsum("mkc,mhc->kh", gdec, hid1, preferred_element_type=f32)
    g_hid1 = jnp.einsum("kh,mkc->mhc", w_out, gdec, preferred_element_type=f32)
    gpre1 = activate_back(pre1, g_hid1).astype(jnp.bfloat16)
    g_in = jnp.einsum("mhc,mfc->hf", gpre1, zin, preferred_element_type=f32)
    grad_latent = jnp.einsum("hf,mhc->mfc", w_in, gpre1, preferred_element_type=f32)
    g_in, g_out, g_close_in, g_close_out = lax.psum(
        (g_in, g_out, g_close_in, g_close_out), ("ens", "space")
    )
    count = g_in.size + g_out.size + g_close_in.size + g_close_out.size
    squares = (
        jnp.sum(g_in * g_in)
        + jnp.sum(g_out * g_out)
        + jnp.sum(g_close_in * g_close_in)
        + jnp.sum(g_close_out * g_close_out)
    )
    rms = jnp.sqrt(squares / count + 1e-12)
    return (grad_latent, g_in / rms, g_out / rms, g_close_in / rms, g_close_out / rms)


def solution(mesh):
    placed = (
        P("ens", None, "space"),
        P("ens", None, "space"),
        P("ens", "space"),
        P(),
        P(),
        P(),
        P(),
    )
    return jax.shard_map(
        body,
        mesh=mesh,
        in_specs=placed,
        out_specs=(P("ens", None, "space"), P(), P(), P(), P()),
        check_vma=False,
    )
```

profile of v0, /device:TPU:0, one launch (start us, length us, event | category | flops | bytes accessed | tf_op | source)
XLA Modules:
  0.0 469.2 jit_solution(4322245571807078582)
XLA Ops:
  8.1 3.5 fusion.34
  11.6 2.6 copy-done.4
  14.2 2.7 fusion.42
  18.8 2.7 copy-done.3
  21.5 4.0 add_bitcast_fusion
  25.6 14.1 %all_gather.6 = f32[224,1024]{1,0:T(8,128)S(1)} all-gather(f32[56,1024]{1,0:T(8,128)S(1)} %copy-done.8), channel_id=1, replica_groups=mesh['ens'=4,'space'=8] {'ens'}, dimensions={0}, use_global_device_ids=true | all-gather | bytes 1146880 | tf_op jit(solution)/shard_map/all_gather | solution.py:44
  39.7 128.7 %all-gather.2.cloned.1.call-done = f32[16,224,1024]{2,1,0:T(8,128)} async-done(((f32[4,224,1024]{2,1,0:T(8,128)}), f32[16,224,1024]{2,1,0:T(8,128)}) %all-gather.2.cloned.1.call-update) | async-done | bytes 14680080 | tf_op jit(solution)/shard_map/all_gather | solution.py:43
  168.3 120.0 %while.14 = (s32[]{:T(128)}, f32[4,224,1024]{2,1,0:T(8,128)}, f32[16,224,1024]{2,1,0:T(8,128)}, f32[4,224,1024]{2,1,0:T(8,128)}, s32[]{:T(128)}, /*index=5*/s32[]{:T(128)}) while((s32[]{:T(128)}, f32[4,224,1024]{2,1,0:T(8,128)}, f32[16,224,1024]{2,1,0:T(8,128)}, f32[4,224,1024]{2,1,0:T(8,128)}, s32[]{:T(128)}, ...), condition=%wide.region_1.2_spmd.clone, body=%wide.region_0.1_spmd.clone.sunk | while | flops 5505027 | bytes 13762643 | solution.py:28
  169.6 5.2 %select_add_fusion.2 = f32[4,224,1024]{2,1,0:T(8,128)} fusion(f32[4,224,1024]{2,1,0:T(8,128)} %get-tuple-element.156, f32[4,224,1024]{2,1,0:T(8,128)} %get-tuple-element.164, f32[224,1024]{1,0:T(8,128)S(1)} %dynamic-slice_bitcast_fusion.2, pred[]{:T(512)S(6)} %compare.3), kind=kLoop, calls=%fused_computation.clone.1 | loop fusion | flops 5505024 | bytes 11927553 | tf_op jit(solution)/shard_map/while/body/eval_jaxpr/add | solution.py:26
  176.0 6.3 %select_add_fusion.2 = f32[4,224,1024]{2,1,0:T(8,128)} fusion(f32[4,224,1024]{2,1,0:T(8,128)} %get-tuple-element.156, f32[4,224,1024]{2,1,0:T(8,128)} %get-tuple-element.164, f32[224,1024]{1,0:T(8,128)S(1)} %dynamic-slice_bitcast_fusion.2, pred[]{:T(512)S(6)} %compare.3), kind=kLoop, calls=%fused_computation.clone.1 | loop fusion | flops 5505024 | bytes 11927553 | tf_op jit(solution)/shard_map/while/body/eval_jaxpr/add | solution.py:26
  183.6 6.3 %select_add_fusion.2 = f32[4,224,1024]{2,1,0:T(8,128)} fusion(f32[4,224,1024]{2,1,0:T(8,128)} %get-tuple-element.156, f32[4,224,1024]{2,1,0:T(8,128)} %get-tuple-element.164, f32[224,1024]{1,0:T(8,128)S(1)} %dynamic-slice_bitcast_fusion.2, pred[]{:T(512)S(6)} %compare.3), kind=kLoop, calls=%fused_computation.clone.1 | loop fusion | flops 5505024 | bytes 11927553 | tf_op jit(solution)/shard_map/while/body/eval_jaxpr/add | solution.py:26
  191.2 6.3 %select_add_fusion.2 = f32[4,224,1024]{2,1,0:T(8,128)} fusion(f32[4,224,1024]{2,1,0:T(8,128)} %get-tuple-element.156, f32[4,224,1024]{2,1,0:T(8,128)} %get-tuple-element.164, f32[224,1024]{1,0:T(8,128)S(1)} %dynamic-slice_bitcast_fusion.2, pred[]{:T(512)S(6)} %compare.3), kind=kLoop, calls=%fused_computation.clone.1 | loop fusion | flops 5505024 | bytes 11927553 | tf_op jit(solution)/shard_map/while/body/eval_jaxpr/add | solution.py:26
  198.7 6.3 %select_add_fusion.2 = f32[4,224,1024]{2,1,0:T(8,128)} fusion(f32[4,224,1024]{2,1,0:T(8,128)} %get-tuple-element.156, f32[4,224,1024]{2,1,0:T(8,128)} %get-tuple-element.164, f32[224,1024]{1,0:T(8,128)S(1)} %dynamic-slice_bitcast_fusion.2, pred[]{:T(512)S(6)} %compare.3), kind=kLoop, calls=%fused_computation.clone.1 | loop fusion | flops 5505024 | bytes 11927553 | tf_op jit(solution)/shard_map/while/body/eval_jaxpr/add | solution.py:26
  206.3 6.3 %select_add_fusion.2 = f32[4,224,1024]{2,1,0:T(8,128)} fusion(f32[4,224,1024]{2,1,0:T(8,128)} %get-tuple-element.156, f32[4,224,1024]{2,1,0:T(8,128)} %get-tuple-element.164, f32[224,1024]{1,0:T(8,128)S(1)} %dynamic-slice_bitcast_fusion.2, pred[]{:T(512)S(6)} %compare.3), kind=kLoop, calls=%fused_computation.clone.1 | loop fusion | flops 5505024 | bytes 11927553 | tf_op jit(solution)/shard_map/while/body/eval_jaxpr/add | solution.py:26
  213.9 6.3 %select_add_fusion.2 = f32[4,224,1024]{2,1,0:T(8,128)} fusion(f32[4,224,1024]{2,1,0:T(8,128)} %get-tuple-element.156, f32[4,224,1024]{2,1,0:T(8,128)} %get-tuple-element.164, f32[224,1024]{1,0:T(8,128)S(1)} %dynamic-slice_bitcast_fusion.2, pred[]{:T(512)S(6)} %compare.3), kind=kLoop, calls=%fused_computation.clone.1 | loop fusion | flops 5505024 | bytes 11927553 | tf_op jit(solution)/shard_map/while/body/eval_jaxpr/add | solution.py:26
  221.4 6.3 %select_add_fusion.2 = f32[4,224,1024]{2,1,0:T(8,128)} fusion(f32[4,224,1024]{2,1,0:T(8,128)} %get-tuple-element.156, f32[4,224,1024]{2,1,0:T(8,128)} %get-tuple-element.164, f32[224,1024]{1,0:T(8,128)S(1)} %dynamic-slice_bitcast_fusion.2, pred[]{:T(512)S(6)} %compare.3), kind=kLoop, calls=%fused_computation.clone.1 | loop fusion | flops 5505024 | bytes 11927553 | tf_op jit(solution)/shard_map/while/body/eval_jaxpr/add | solution.py:26
  229.0 6.3 %select_add_fusion.2 = f32[4,224,1024]{2,1,0:T(8,128)} fusion(f32[4,224,1024]{2,1,0:T(8,128)} %get-tuple-element.156, f32[4,224,1024]{2,1,0:T(8,128)} %get-tuple-element.164, f32[224,1024]{1,0:T(8,128)S(1)} %dynamic-slice_bitcast_fusion.2, pred[]{:T(512)S(6)} %compare.3), kind=kLoop, calls=%fused_computation.clone.1 | loop fusion | flops 5505024 | bytes 11927553 | tf_op jit(solution)/shard_map/while/body/eval_jaxpr/add | solution.py:26
  236.6 6.3 %select_add_fusion.2 = f32[4,224,1024]{2,1,0:T(8,128)} fusion(f32[4,224,1024]{2,1,0:T(8,128)} %get-tuple-element.156, f32[4,224,1024]{2,1,0:T(8,128)} %get-tuple-element.164, f32[224,1024]{1,0:T(8,128)S(1)} %dynamic-slice_bitcast_fusion.2, pred[]{:T(512)S(6)} %compare.3), kind=kLoop, calls=%fused_computation.clone.1 | loop fusion | flops 5505024 | bytes 11927553 | tf_op jit(solution)/shard_map/while/body/eval_jaxpr/add | solution.py:26
  244.2 6.3 %select_add_fusion.2 = f32[4,224,1024]{2,1,0:T(8,128)} fusion(f32[4,224,1024]{2,1,0:T(8,128)} %get-tuple-element.156, f32[4,224,1024]{2,1,0:T(8,128)} %get-tuple-element.164, f32[224,1024]{1,0:T(8,128)S(1)} %dynamic-slice_bitcast_fusion.2, pred[]{:T(512)S(6)} %compare.3), kind=kLoop, calls=%fused_computation.clone.1 | loop fusion | flops 5505024 | bytes 11927553 | tf_op jit(solution)/shard_map/while/body/eval_jaxpr/add | solution.py:26
  251.7 6.3 %select_add_fusion.2 = f32[4,224,1024]{2,1,0:T(8,128)} fusion(f32[4,224,1024]{2,1,0:T(8,128)} %get-tuple-element.156, f32[4,224,1024]{2,1,0:T(8,128)} %get-tuple-element.164, f32[224,1024]{1,0:T(8,128)S(1)} %dynamic-slice_bitcast_fusion.2, pred[]{:T(512)S(6)} %compare.3), kind=kLoop, calls=%fused_computation.clone.1 | loop fusion | flops 5505024 | bytes 11927553 | tf_op jit(solution)/shard_map/while/body/eval_jaxpr/add | solution.py:26
  259.3 6.3 %select_add_fusion.2 = f32[4,224,1024]{2,1,0:T(8,128)} fusion(f32[4,224,1024]{2,1,0:T(8,128)} %get-tuple-element.156, f32[4,224,1024]{2,1,0:T(8,128)} %get-tuple-element.164, f32[224,1024]{1,0:T(8,128)S(1)} %dynamic-slice_bitcast_fusion.2, pred[]{:T(512)S(6)} %compare.3), kind=kLoop, calls=%fused_computation.clone.1 | loop fusion | flops 5505024 | bytes 11927553 | tf_op jit(solution)/shard_map/while/body/eval_jaxpr/add | solution.py:26
  266.9 6.3 %select_add_fusion.2 = f32[4,224,1024]{2,1,0:T(8,128)} fusion(f32[4,224,1024]{2,1,0:T(8,128)} %get-tuple-element.156, f32[4,224,1024]{2,1,0:T(8,128)} %get-tuple-element.164, f32[224,1024]{1,0:T(8,128)S(1)} %dynamic-slice_bitcast_fusion.2, pred[]{:T(512)S(6)} %compare.3), kind=kLoop, calls=%fused_computation.clone.1 | loop fusion | flops 5505024 | bytes 11927553 | tf_op jit(solution)/shard_map/while/body/eval_jaxpr/add | solution.py:26
  274.4 6.3 %select_add_fusion.2 = f32[4,224,1024]{2,1,0:T(8,128)} fusion(f32[4,224,1024]{2,1,0:T(8,128)} %get-tuple-element.156, f32[4,224,1024]{2,1,0:T(8,128)} %get-tuple-element.164, f32[224,1024]{1,0:T(8,128)S(1)} %dynamic-slice_bitcast_fusion.2, pred[]{:T(512)S(6)} %compare.3), kind=kLoop, calls=%fused_computation.clone.1 | loop fusion | flops 5505024 | bytes 11927553 | tf_op jit(solution)/shard_map/while/body/eval_jaxpr/add | solution.py:26
  282.0 6.3 %select_add_fusion.2 = f32[4,224,1024]{2,1,0:T(8,128)} fusion(f32[4,224,1024]{2,1,0:T(8,128)} %get-tuple-element.156, f32[4,224,1024]{2,1,0:T(8,128)} %get-tuple-element.164, f32[224,1024]{1,0:T(8,128)S(1)} %dynamic-slice_bitcast_fusion.2, pred[]{:T(512)S(6)} %compare.3), kind=kLoop, calls=%fused_computation.clone.1 | loop fusion | flops 5505024 | bytes 11927553 | tf_op jit(solution)/shard_map/while/body/eval_jaxpr/add | solution.py:26
  288.3 4.3 multiply_subtract_fusion
  293.3 4.8 %fusion.13 = bf16[4,384,1024]{1,2,0:T(8,128)(2,1)S(1)} fusion(f32[4,1024,384]{2,1,0:T(8,128)S(1)} %bitcast.110, f32[4,224,1024]{2,1,0:T(8,128)S(1)} %multiply_subtract_fusion, bf16[224,384]{1,0:T(8,128)(2,1)S(1)} %copy-done.9), kind=kOutput, calls=%fused_computation.19 | convolution fusion | flops 737017856 | bytes 13279232 | tf_op jit(solution)/shard_map/kh,mkc->mhc/dot_general | solution.py:49
  299.5 3.2 convolution_bitcast_fusion.3
  302.7 5.0 %fusion.6 = bf16[4,384,1024]{1,2,0:T(8,128)(2,1)S(1)} fusion(f32[4,1024,384]{2,1,0:T(8,128)S(1)} %bitcast.112, bf16[4,224,1024]{2,1,0:T(8,128)(2,1)S(1)} %fusion.22, bf16[224,384]{1,0:T(8,128)(2,1)S(1)} %copy-done.10), kind=kOutput, calls=%fused_computation.12 | convolution fusion | flops 736100352 | bytes 11444224 | tf_op jit(solution)/shard_map/kh,mkc->mhc/dot_general | solution.py:56
  309.6 3.1 convolution_bitcast_fusion.2
  314.7 3.2 convolution_bitcast_fusion
  317.9 5.4 %copy.29 = f32[4,256,1024]{2,1,0:T(8,128)} copy(f32[4,256,1024]{1,2,0:T(8,128)} %convolution_bitcast_fusion) | data formatting | bytes 8388608
  323.2 124.4 %all-reduce.3.cloned.1.call-done = (f32[384,256]{1,0:T(8,128)}, f32[224,384]{1,0:T(8,128)}, f32[384,224]{0,1:T(8,128)}, f32[224,384]{1,0:T(8,128)}) async-done(((f32[384,256]{1,0:T(8,128)}, f32[224,384]{1,0:T(8,128)}, f32[384,224]{0,1:T(8,128)}, f32[224,384]{1,0:T(8,128)}), (f32[384,256]{1,0:T(8,128)}, f32[224,384]{1,0:T(8,128)}, f32[384,224]{0,1:T(8,128)}, ...) | async-done | bytes 1425424 | tf_op jit(solution)/shard_map/psum | solution.py:60
  (62 shorter events, 40.6 us)
Async XLA Ops:
  7.2 0.9 copy-start
  7.2 7.0 %copy-start.10 = (bf16[224,384]{1,0:T(8,128)(2,1)S(1)}, bf16[224,384]{1,0:T(8,128)(2,1)}, u32[]{:S(2)}) copy-start(bf16[224,384]{1,0:T(8,128)(2,1)} %param.13) | copy-start | bytes 516100
  7.2 161.1 %all-gather.2.cloned.1.call-start = ((), (), s32[]{:S(2)}) async-start(), calls=%async_computation | async-start | bytes 18350080 | tf_op jit(solution)/shard_map/all_gather | solution.py:43
  11.6 2.6 copy-start.4
  14.2 2.7 copy-start.7
  16.9 1.9 copy-start.1
  16.9 4.5 copy-start.9
  18.8 2.7 copy-start.3
  21.5 4.1 copy-start.8
  25.5 422.1 %all-reduce.3.cloned.1.call-start = ((), (), s32[]{:S(2)}) async-start(), calls=%async_computation.1 | async-start | bytes 2850816 | tf_op jit(solution)/shard_map/psum | solution.py:60
  288.3 4.4 slice-start
  288.3 5.0 %slice-start.1 = ((s8[6291456]{0:T(1024)(128)(4,1)}), s8[2097152]{0:T(1024)(128)(4,1)S(1)}, s32[]{:S(2)}) async-start(s8[6291456]{0:T(1024)(128)(4,1)} %bitcast.109), calls=%async_computation.3 | async-start | bytes 4194304
  288.3 11.1 %slice-start.2 = ((s8[6291456]{0:T(1024)(128)(4,1)}), s8[4194304]{0:T(1024)(128)(4,1)S(1)}, s32[]{:S(2)}) async-start(s8[6291456]{0:T(1024)(128)(4,1)} %bitcast.111), calls=%async_computation.4 | async-start | bytes 8388608
  293.3 6.1 %slice-start.3 = ((s8[6291456]{0:T(1024)(128)(4,1)}), s8[2097152]{0:T(1024)(128)(4,1)S(1)}, s32[]{:S(2)}) async-start(s8[6291456]{0:T(1024)(128)(4,1)} %bitcast.111), calls=%async_computation.5 | async-start | bytes 4194304
  302.7 5.0 %copy-start.2 = (f32[4,1024,224]{1,2,0:T(8,128)S(1)}, f32[4,1024,224]{1,2,0:T(8,128)}, u32[]{:S(2)}) copy-start(f32[4,1024,224]{1,2,0:T(8,128)} %copy-done.1) | copy-start | bytes 11010052
  309.6 3.2 copy-start.5
  309.6 3.2 copy-start.6
Sparse Core Ops, SparseCore 0:
  25.6 142.6 all-gather.1
  314.8 132.7 all-reduce.2
where the time goes:
time: 470 us; the launch traced here: 469 us
  waiting for transfers between devices  253 us (54%)
  other arithmetic  116 us (25%)
  matrix products  36 us (8%)
  local copies, waits for them, and re-layouts  32.5 us (7%)
  between operations  16.8 us (4%)
  blocking collectives  14.1 us (3%)
    all_gather x1, waiting for transfers between devices, body(): lax.all_gather(pred, 'ens', axis=0, tiled=True)  129 us
    psum x1, waiting for transfers between devices, body(): lax.psum((g_in, g_out, g_close_in, g_close_out), ('ens', 'space'))  124 us
    add x16, other arithmetic, add_one(): return total + smooth_sign(mine - other)  100 us
    sub x16, local copies, waits for them, and re-layouts, add_one(): return total + smooth_sign(mine - other)  19.8 us
    all_gather x1, blocking collectives, body(): lax.all_gather(target, 'ens', axis=0, tiled=True)  14.1 us
    unnamed x31, local copies, waits for them, and re-layouts  12.7 us
  transfers between devices with their start and end apart: 2, of which 2 were waited for; matrix products, arithmetic and copies ran while one was open for 2% of the time, Pallas kernels for 0%

commit v1 on v0

--- a/solution.py
+++ b/solution.py
@@ -58,7 +58,7 @@
     g_in = jnp.einsum("mhc,mfc->hf", gpre1, zin, preferred_element_type=f32)
     grad_latent = jnp.einsum("hf,mhc->mfc", w_in, gpre1, preferred_element_type=f32)
     g_in, g_out, g_close_in, g_close_out = lax.psum(
-        (g_in, g_out, g_close_in, g_close_out), ("ens", "space")
+        lax.psum((g_in, g_out, g_close_in, g_close_out), "space"), "ens"
     )
     count = g_in.size + g_out.size + g_close_in.size + g_close_out.size
     squares = (

time: 470 us -> 460 us (0.979)
  waiting for transfers between devices: 253 us -> 243 us
    psum x1 -> x2, waiting for transfers between devices: 124 us -> 114 us  [the longest x1 61.2 us: body(): lax.psum((g_in, g_out, g_close_in, g_close_out), 'space')]
  transfers between devices with their start and end apart: 2 -> 3, of which waited for: 2 -> 3; matrix products, arithmetic and copies ran while one was open for 2% -> 2% of each run, Pallas kernels for 0% -> 0%
where the time goes in v1:
time: 460 us; the launch traced here: 459 us
  waiting for transfers between devices  243 us (53%)
  other arithmetic  116 us (25%)
  matrix products  36 us (8%)
  local copies, waits for them, and re-layouts  32.5 us (7%)
  between operations  16.5 us (4%)
  blocking collectives  14.1 us (3%)
    all_gather x1, waiting for transfers between devices, body(): lax.all_gather(pred, 'ens', axis=0, tiled=True)  129 us
    add x16, other arithmetic, add_one(): return total + smooth_sign(mine - other)  100 us
    psum x1, waiting for transfers between devices, body(): lax.psum((g_in, g_out, g_close_in, g_close_out), 'space')  61.2 us
    psum x1, waiting for transfers between devices, body(): lax.psum(lax.psum((g_in, g_out, g_close_in, g_close_out), 'space'), 'ens')  53.2 us
    sub x16, local copies, waits for them, and re-layouts, add_one(): return total + smooth_sign(mine - other)  19.8 us
    all_gather x1, blocking collectives, body(): lax.all_gather(target, 'ens', axis=0, tiled=True)  14.1 us
    unnamed x31, local copies, waits for them, and re-layouts  12.7 us
  transfers between devices with their start and end apart: 3, of which 3 were waited for; matrix products, arithmetic and copies ran while one was open for 2% of the time, Pallas kernels for 0%

profile of v1, /device:TPU:0, one launch (start us, length us, event | category | flops | bytes accessed | tf_op | source)
XLA Modules:
  0.0 459.1 jit_solution(11918158029717087061)
XLA Ops:
  8.1 3.5 fusion.34
  14.2 2.7 fusion.42
  18.9 2.6 copy-done.3
  21.5 4.0 add_bitcast_fusion
  25.6 14.1 %all_gather.6 = f32[224,1024]{1,0:T(8,128)S(1)} all-gather(f32[56,1024]{1,0:T(8,128)S(1)} %copy-done.8), channel_id=1, replica_groups=mesh['ens'=4,'space'=8] {'ens'}, dimensions={0}, use_global_device_ids=true | all-gather | bytes 1146880 | tf_op jit(solution)/shard_map/all_gather | solution.py:44
  39.7 128.7 %all-gather.2.cloned.1.call-done = f32[16,224,1024]{2,1,0:T(8,128)} async-done(((f32[4,224,1024]{2,1,0:T(8,128)}), f32[16,224,1024]{2,1,0:T(8,128)}) %all-gather.2.cloned.1.call-update) | async-done | bytes 14680080 | tf_op jit(solution)/shard_map/all_gather | solution.py:43
  168.4 120.0 %while.14 = (s32[]{:T(128)}, f32[4,224,1024]{2,1,0:T(8,128)}, f32[16,224,1024]{2,1,0:T(8,128)}, f32[4,224,1024]{2,1,0:T(8,128)}, s32[]{:T(128)}, /*index=5*/s32[]{:T(128)}) while((s32[]{:T(128)}, f32[4,224,1024]{2,1,0:T(8,128)}, f32[16,224,1024]{2,1,0:T(8,128)}, f32[4,224,1024]{2,1,0:T(8,128)}, s32[]{:T(128)}, ...), condition=%wide.region_1.2_spmd.clone, body=%wide.region_0.1_spmd.clone.sunk | while | flops 5505027 | bytes 13762643 | solution.py:28
  169.6 5.2 %select_add_fusion.2 = f32[4,224,1024]{2,1,0:T(8,128)} fusion(f32[4,224,1024]{2,1,0:T(8,128)} %get-tuple-element.160, f32[4,224,1024]{2,1,0:T(8,128)} %get-tuple-element.168, f32[224,1024]{1,0:T(8,128)S(1)} %dynamic-slice_bitcast_fusion.2, pred[]{:T(512)S(6)} %compare.3), kind=kLoop, calls=%fused_computation.clone.1 | loop fusion | flops 5505024 | bytes 11927553 | tf_op jit(solution)/shard_map/while/body/eval_jaxpr/add | solution.py:26
  176.1 6.3 %select_add_fusion.2 = f32[4,224,1024]{2,1,0:T(8,128)} fusion(f32[4,224,1024]{2,1,0:T(8,128)} %get-tuple-element.160, f32[4,224,1024]{2,1,0:T(8,128)} %get-tuple-element.168, f32[224,1024]{1,0:T(8,128)S(1)} %dynamic-slice_bitcast_fusion.2, pred[]{:T(512)S(6)} %compare.3), kind=kLoop, calls=%fused_computation.clone.1 | loop fusion | flops 5505024 | bytes 11927553 | tf_op jit(solution)/shard_map/while/body/eval_jaxpr/add | solution.py:26
  183.6 6.3 %select_add_fusion.2 = f32[4,224,1024]{2,1,0:T(8,128)} fusion(f32[4,224,1024]{2,1,0:T(8,128)} %get-tuple-element.160, f32[4,224,1024]{2,1,0:T(8,128)} %get-tuple-element.168, f32[224,1024]{1,0:T(8,128)S(1)} %dynamic-slice_bitcast_fusion.2, pred[]{:T(512)S(6)} %compare.3), kind=kLoop, calls=%fused_computation.clone.1 | loop fusion | flops 5505024 | bytes 11927553 | tf_op jit(solution)/shard_map/while/body/eval_jaxpr/add | solution.py:26
  191.2 6.3 %select_add_fusion.2 = f32[4,224,1024]{2,1,0:T(8,128)} fusion(f32[4,224,1024]{2,1,0:T(8,128)} %get-tuple-element.160, f32[4,224,1024]{2,1,0:T(8,128)} %get-tuple-element.168, f32[224,1024]{1,0:T(8,128)S(1)} %dynamic-slice_bitcast_fusion.2, pred[]{:T(512)S(6)} %compare.3), kind=kLoop, calls=%fused_computation.clone.1 | loop fusion | flops 5505024 | bytes 11927553 | tf_op jit(solution)/shard_map/while/body/eval_jaxpr/add | solution.py:26
  198.8 6.3 %select_add_fusion.2 = f32[4,224,1024]{2,1,0:T(8,128)} fusion(f32[4,224,1024]{2,1,0:T(8,128)} %get-tuple-element.160, f32[4,224,1024]{2,1,0:T(8,128)} %get-tuple-element.168, f32[224,1024]{1,0:T(8,128)S(1)} %dynamic-slice_bitcast_fusion.2, pred[]{:T(512)S(6)} %compare.3), kind=kLoop, calls=%fused_computation.clone.1 | loop fusion | flops 5505024 | bytes 11927553 | tf_op jit(solution)/shard_map/while/body/eval_jaxpr/add | solution.py:26
  206.3 6.3 %select_add_fusion.2 = f32[4,224,1024]{2,1,0:T(8,128)} fusion(f32[4,224,1024]{2,1,0:T(8,128)} %get-tuple-element.160, f32[4,224,1024]{2,1,0:T(8,128)} %get-tuple-element.168, f32[224,1024]{1,0:T(8,128)S(1)} %dynamic-slice_bitcast_fusion.2, pred[]{:T(512)S(6)} %compare.3), kind=kLoop, calls=%fused_computation.clone.1 | loop fusion | flops 5505024 | bytes 11927553 | tf_op jit(solution)/shard_map/while/body/eval_jaxpr/add | solution.py:26
  213.9 6.3 %select_add_fusion.2 = f32[4,224,1024]{2,1,0:T(8,128)} fusion(f32[4,224,1024]{2,1,0:T(8,128)} %get-tuple-element.160, f32[4,224,1024]{2,1,0:T(8,128)} %get-tuple-element.168, f32[224,1024]{1,0:T(8,128)S(1)} %dynamic-slice_bitcast_fusion.2, pred[]{:T(512)S(6)} %compare.3), kind=kLoop, calls=%fused_computation.clone.1 | loop fusion | flops 5505024 | bytes 11927553 | tf_op jit(solution)/shard_map/while/body/eval_jaxpr/add | solution.py:26
  221.5 6.3 %select_add_fusion.2 = f32[4,224,1024]{2,1,0:T(8,128)} fusion(f32[4,224,1024]{2,1,0:T(8,128)} %get-tuple-element.160, f32[4,224,1024]{2,1,0:T(8,128)} %get-tuple-element.168, f32[224,1024]{1,0:T(8,128)S(1)} %dynamic-slice_bitcast_fusion.2, pred[]{:T(512)S(6)} %compare.3), kind=kLoop, calls=%fused_computation.clone.1 | loop fusion | flops 5505024 | bytes 11927553 | tf_op jit(solution)/shard_map/while/body/eval_jaxpr/add | solution.py:26
  229.1 6.3 %select_add_fusion.2 = f32[4,224,1024]{2,1,0:T(8,128)} fusion(f32[4,224,1024]{2,1,0:T(8,128)} %get-tuple-element.160, f32[4,224,1024]{2,1,0:T(8,128)} %get-tuple-element.168, f32[224,1024]{1,0:T(8,128)S(1)} %dynamic-slice_bitcast_fusion.2, pred[]{:T(512)S(6)} %compare.3), kind=kLoop, calls=%fused_computation.clone.1 | loop fusion | flops 5505024 | bytes 11927553 | tf_op jit(solution)/shard_map/while/body/eval_jaxpr/add | solution.py:26
  236.6 6.3 %select_add_fusion.2 = f32[4,224,1024]{2,1,0:T(8,128)} fusion(f32[4,224,1024]{2,1,0:T(8,128)} %get-tuple-element.160, f32[4,224,1024]{2,1,0:T(8,128)} %get-tuple-element.168, f32[224,1024]{1,0:T(8,128)S(1)} %dynamic-slice_bitcast_fusion.2, pred[]{:T(512)S(6)} %compare.3), kind=kLoop, calls=%fused_computation.clone.1 | loop fusion | flops 5505024 | bytes 11927553 | tf_op jit(solution)/shard_map/while/body/eval_jaxpr/add | solution.py:26
  244.2 6.3 %select_add_fusion.2 = f32[4,224,1024]{2,1,0:T(8,128)} fusion(f32[4,224,1024]{2,1,0:T(8,128)} %get-tuple-element.160, f32[4,224,1024]{2,1,0:T(8,128)} %get-tuple-element.168, f32[224,1024]{1,0:T(8,128)S(1)} %dynamic-slice_bitcast_fusion.2, pred[]{:T(512)S(6)} %compare.3), kind=kLoop, calls=%fused_computation.clone.1 | loop fusion | flops 5505024 | bytes 11927553 | tf_op jit(solution)/shard_map/while/body/eval_jaxpr/add | solution.py:26
  251.8 6.3 %select_add_fusion.2 = f32[4,224,1024]{2,1,0:T(8,128)} fusion(f32[4,224,1024]{2,1,0:T(8,128)} %get-tuple-element.160, f32[4,224,1024]{2,1,0:T(8,128)} %get-tuple-element.168, f32[224,1024]{1,0:T(8,128)S(1)} %dynamic-slice_bitcast_fusion.2, pred[]{:T(512)S(6)} %compare.3), kind=kLoop, calls=%fused_computation.clone.1 | loop fusion | flops 5505024 | bytes 11927553 | tf_op jit(solution)/shard_map/while/body/eval_jaxpr/add | solution.py:26
  259.3 6.3 %select_add_fusion.2 = f32[4,224,1024]{2,1,0:T(8,128)} fusion(f32[4,224,1024]{2,1,0:T(8,128)} %get-tuple-element.160, f32[4,224,1024]{2,1,0:T(8,128)} %get-tuple-element.168, f32[224,1024]{1,0:T(8,128)S(1)} %dynamic-slice_bitcast_fusion.2, pred[]{:T(512)S(6)} %compare.3), kind=kLoop, calls=%fused_computation.clone.1 | loop fusion | flops 5505024 | bytes 11927553 | tf_op jit(solution)/shard_map/while/body/eval_jaxpr/add | solution.py:26
  266.9 6.3 %select_add_fusion.2 = f32[4,224,1024]{2,1,0:T(8,128)} fusion(f32[4,224,1024]{2,1,0:T(8,128)} %get-tuple-element.160, f32[4,224,1024]{2,1,0:T(8,128)} %get-tuple-element.168, f32[224,1024]{1,0:T(8,128)S(1)} %dynamic-slice_bitcast_fusion.2, pred[]{:T(512)S(6)} %compare.3), kind=kLoop, calls=%fused_computation.clone.1 | loop fusion | flops 5505024 | bytes 11927553 | tf_op jit(solution)/shard_map/while/body/eval_jaxpr/add | solution.py:26
  274.5 6.3 %select_add_fusion.2 = f32[4,224,1024]{2,1,0:T(8,128)} fusion(f32[4,224,1024]{2,1,0:T(8,128)} %get-tuple-element.160, f32[4,224,1024]{2,1,0:T(8,128)} %get-tuple-element.168, f32[224,1024]{1,0:T(8,128)S(1)} %dynamic-slice_bitcast_fusion.2, pred[]{:T(512)S(6)} %compare.3), kind=kLoop, calls=%fused_computation.clone.1 | loop fusion | flops 5505024 | bytes 11927553 | tf_op jit(solution)/shard_map/while/body/eval_jaxpr/add | solution.py:26
  282.0 6.3 %select_add_fusion.2 = f32[4,224,1024]{2,1,0:T(8,128)} fusion(f32[4,224,1024]{2,1,0:T(8,128)} %get-tuple-element.160, f32[4,224,1024]{2,1,0:T(8,128)} %get-tuple-element.168, f32[224,1024]{1,0:T(8,128)S(1)} %dynamic-slice_bitcast_fusion.2, pred[]{:T(512)S(6)} %compare.3), kind=kLoop, calls=%fused_computation.clone.1 | loop fusion | flops 5505024 | bytes 11927553 | tf_op jit(solution)/shard_map/while/body/eval_jaxpr/add | solution.py:26
  288.4 4.3 multiply_subtract_fusion
  293.4 4.8 %fusion.13 = bf16[4,384,1024]{1,2,0:T(8,128)(2,1)S(1)} fusion(f32[4,1024,384]{2,1,0:T(8,128)S(1)} %bitcast.110, f32[4,224,1024]{2,1,0:T(8,128)S(1)} %multiply_subtract_fusion, bf16[224,384]{1,0:T(8,128)(2,1)S(1)} %copy-done.9), kind=kOutput, calls=%fused_computation.19 | convolution fusion | flops 737017856 | bytes 13279232 | tf_op jit(solution)/shard_map/kh,mkc->mhc/dot_general | solution.py:49
  299.5 3.2 convolution_bitcast_fusion.3
  302.7 5.0 %fusion.6 = bf16[4,384,1024]{1,2,0:T(8,128)(2,1)S(1)} fusion(f32[4,1024,384]{2,1,0:T(8,128)S(1)} %bitcast.112, bf16[4,224,1024]{2,1,0:T(8,128)(2,1)S(1)} %fusion.22, bf16[224,384]{1,0:T(8,128)(2,1)S(1)} %copy-done.10), kind=kOutput, calls=%fused_computation.12 | convolution fusion | flops 736100352 | bytes 11444224 | tf_op jit(solution)/shard_map/kh,mkc->mhc/dot_general | solution.py:56
  309.7 3.1 convolution_bitcast_fusion.2
  314.8 61.2 %all-reduce.5.cloned.1.call-done = (f32[384,256]{1,0:T(8,128)}, f32[224,384]{1,0:T(8,128)}, f32[384,224]{0,1:T(8,128)}, f32[224,384]{1,0:T(8,128)}) async-done(((f32[384,256]{1,0:T(8,128)}, f32[224,384]{1,0:T(8,128)}, f32[384,224]{0,1:T(8,128)}, f32[224,384]{1,0:T(8,128)}), (f32[384,256]{1,0:T(8,128)}, f32[224,384]{1,0:T(8,128)}, f32[384,224]{0,1:T(8,128)}, ...) | async-done | bytes 1425424 | tf_op jit(solution)/shard_map/psum | solution.py:61
  376.0 3.2 convolution_bitcast_fusion
  379.3 5.3 %copy.29 = f32[4,256,1024]{2,1,0:T(8,128)} copy(f32[4,256,1024]{1,2,0:T(8,128)} %convolution_bitcast_fusion) | data formatting | bytes 8388608
  384.6 53.2 %all-reduce.7.cloned.1.call-done = (f32[384,256]{1,0:T(8,128)}, f32[224,384]{1,0:T(8,128)}, f32[384,224]{0,1:T(8,128)}, f32[224,384]{1,0:T(8,128)}) async-done(((f32[384,256]{1,0:T(8,128)}, f32[224,384]{1,0:T(8,128)}, f32[384,224]{0,1:T(8,128)}, f32[224,384]{1,0:T(8,128)}), (f32[384,256]{1,0:T(8,128)}, f32[224,384]{1,0:T(8,128)}, f32[384,224]{0,1:T(8,128)}, ...) | async-done | bytes 1425424 | tf_op jit(solution)/shard_map/psum | solution.py:60
  (65 shorter events, 43.2 us)
Async XLA Ops:
  7.2 0.9 copy-start
  7.2 7.0 %copy-start.10 = (bf16[224,384]{1,0:T(8,128)(2,1)S(1)}, bf16[224,384]{1,0:T(8,128)(2,1)}, u32[]{:S(2)}) copy-start(bf16[224,384]{1,0:T(8,128)(2,1)} %param.13) | copy-start | bytes 516100
  7.2 161.2 %all-gather.2.cloned.1.call-start = ((), (), s32[]{:S(2)}) async-start(), calls=%async_computation | async-start | bytes 18350080 | tf_op jit(solution)/shard_map/all_gather | solution.py:43
  11.6 2.6 copy-start.4
  14.2 2.7 copy-start.7
  16.9 1.9 copy-start.1
  16.9 4.6 copy-start.9
  18.9 2.6 copy-start.3
  21.5 4.1 copy-start.8
  25.5 350.5 %all-reduce.5.cloned.1.call-start = ((), (), s32[]{:S(2)}) async-start(), calls=%async_computation.1 | async-start | bytes 2850816 | tf_op jit(solution)/shard_map/psum | solution.py:61
  288.4 4.4 slice-start
  288.4 5.0 %slice-start.1 = ((s8[6291456]{0:T(1024)(128)(4,1)}), s8[2097152]{0:T(1024)(128)(4,1)S(1)}, s32[]{:S(2)}) async-start(s8[6291456]{0:T(1024)(128)(4,1)} %bitcast.109), calls=%async_computation.4 | async-start | bytes 4194304
  288.4 11.1 %slice-start.2 = ((s8[6291456]{0:T(1024)(128)(4,1)}), s8[4194304]{0:T(1024)(128)(4,1)S(1)}, s32[]{:S(2)}) async-start(s8[6291456]{0:T(1024)(128)(4,1)} %bitcast.111), calls=%async_computation.5 | async-start | bytes 8388608
  293.4 6.1 %slice-start.3 = ((s8[6291456]{0:T(1024)(128)(4,1)}), s8[2097152]{0:T(1024)(128)(4,1)S(1)}, s32[]{:S(2)}) async-start(s8[6291456]{0:T(1024)(128)(4,1)} %bitcast.111), calls=%async_computation.6 | async-start | bytes 4194304
  302.7 5.0 %copy-start.2 = (f32[4,1024,224]{1,2,0:T(8,128)S(1)}, f32[4,1024,224]{1,2,0:T(8,128)}, u32[]{:S(2)}) copy-start(f32[4,1024,224]{1,2,0:T(8,128)} %copy-done.1) | copy-start | bytes 11010052
  309.7 3.2 copy-start.5
  309.7 3.2 copy-start.6
  314.7 123.1 %all-reduce.7.cloned.1.call-start = ((), (), s32[]{:S(2)}) async-start(), calls=%async_computation.2 | async-start | bytes 2850816 | tf_op jit(solution)/shard_map/psum | solution.py:60
Sparse Core Ops, SparseCore 0:
  25.7 142.6 all-gather.1
  314.8 61.1 all-reduce.4
  379.5 58.3 all-reduce.6
